TPU v7x, 256 devices: a whole 4x4x8 slice. The times are simulated.
256 devices in a mesh: gz: 8 (over x, core), gx: 32 (over z, y).
Axes of the slice: x: 4, y: 4, z: 8, core: 2. Of those that a mesh axis runs over, the one named last changes fastest.
Arguments:
- volume: float32 [256, 512, 256], P('gz', 'gx')
- measured: float32 [2, 256, 2048], P(None, 'gz')
- weight_blocks: bfloat16 [64, 128, 128], replicated, may hold values from 0 to 2
- view_order: int32 [2], replicated, may hold values from 0 to 1, each once
- tile_voxel: int32 [2, 8, 16384], P(None, 'gz', 'gx'), may hold values from 0 to 1023
- tile_column: int32 [2, 8, 16384], P(None, 'gz', 'gx'), may hold values from 0 to 15
- tile_block: int32 [2, 8, 16384], P(None, 'gz', 'gx'), may hold values from 0 to 63
- entry_count: int32 [2, 8, 32], P(None, 'gz', 'gx'), may hold values from 1 to 512, as said below
Outputs:
- volume_out: float32 [256, 512, 256], P('gz', 'gx')
Inputs may be any that keep to these rules, and one draw needn't show every extreme that they name: Entries of block (a, c) of view v at or past entry_count[v, a, c] are not used; in every view some block has 512 live entries.
All inputs are finite; a program needn't handle non-finite values.
Results may differ from a plain program's by a relative error of at most 0.0027.
Values may be sent and summed in bfloat16 or wider, within the bound.
A program may use at most 64 MiB of HBM per device.

v0:
```python
import jax
import jax.numpy as jnp
from jax import lax
from jax.sharding import PartitionSpec as P

TV_STEPS = 4
smooth_floor = 0.01
step_gain = 0.25
norm_floor = 1e-06
group_rows = 128


def padded_2(cells, sides, width):
    for axis, dim in sides:
        count = lax.axis_size(axis)
        ends = count - 1
        head = lax.slice_in_dim(cells, 0, width, axis=dim)
        tail = lax.slice_in_dim(cells, cells.shape[dim] - width, cells.shape[dim], axis=dim)
        cells = jnp.concatenate(
            [
                lax.ppermute(tail, axis, [(i, (i + 1) % count) for i in range(ends)]),
                cells,
                lax.ppermute(head, axis, [((i + 1) % count, i) for i in range(ends)]),
            ],
            axis=dim,
        )
    return cells


def tv_grad(padded):
    base_cells = padded[:-1, :-1, :-1]
    diff_z = padded[1:, :-1, :-1] - base_cells
    diff_x = padded[:-1, 1:, :-1] - base_cells
    diff_y = padded[:-1, :-1, 1:] - base_cells
    inverse = lax.rsqrt(diff_z * diff_z + diff_x * diff_x + diff_y * diff_y + smooth_floor)
    flow_z = diff_z * inverse
    flow_x = diff_x * inverse
    flow_y = diff_y * inverse
    flow_all = flow_z + flow_x + flow_y
    return flow_z[:-1, 1:, 1:] + flow_x[1:, :-1, 1:] + flow_y[1:, 1:, :-1] - flow_all[1:, 1:, 1:]


def pad_depth(field):
    return jnp.pad(field, ((0, 0), (0, 0), (1, 1)))


def body(
    volume, measured, weight_blocks, view_order, tile_voxel, tile_column, tile_block, entry_count
):
    depth_z, depth_x, depth_y = volume.shape
    tiles_y = depth_y // group_rows
    tiles_u = measured.shape[2] // group_rows
    slab_tiles = depth_z * tiles_u
    plane_tiles = depth_x * tiles_y
    row_weight = jnp.sum(weight_blocks, axis=2, dtype=jnp.float32)
    col_weight = jnp.sum(weight_blocks, axis=1, dtype=jnp.float32)
    offsets = jnp.arange(group_rows, dtype=jnp.int32)
    current = volume
    for turn_index in range(view_order.shape[0]):
        view_index = view_order[turn_index]
        voxel_list = lax.dynamic_index_in_dim(tile_voxel, view_index, 0, keepdims=False)[0]
        column_list = lax.dynamic_index_in_dim(tile_column, view_index, 0, keepdims=False)[0]
        block_list = lax.dynamic_index_in_dim(tile_block, view_index, 0, keepdims=False)[0]
        live_count = lax.dynamic_index_in_dim(entry_count, view_index, 0, keepdims=False)[0, 0]
        rounds = (live_count + group_rows - 1) // group_rows
        voxel_tiles = current.astype(jnp.bfloat16).reshape(-1, group_rows)

        def gather_group(index):
            begin = index * group_rows
            voxels = lax.dynamic_slice_in_dim(voxel_list, begin, group_rows)
            columns = lax.dynamic_slice_in_dim(column_list, begin, group_rows)
            chosen = lax.dynamic_slice_in_dim(block_list, begin, group_rows)
            weight = (begin + offsets < live_count).astype(jnp.float32)[:, None]
            detector = voxels // plane_tiles * tiles_u + columns
            return (voxels, detector, chosen, weight)

        def forward(index, carry):
            projection, ray_sum = carry
            voxels, detector, chosen, weight = gather_group(index)
            product = jnp.einsum(
                "ejk,ek->ej",
                weight_blocks[chosen],
                voxel_tiles[voxels],
                preferred_element_type=jnp.float32,
            )
            return (
                projection.at[detector].add(product * weight),
                ray_sum.at[detector].add(row_weight[chosen] * weight),
            )

        empty = jnp.zeros((slab_tiles, group_rows), jnp.float32)
        projection, ray_sum = lax.fori_loop(0, rounds, forward, (empty, empty))
        target = lax.dynamic_index_in_dim(measured, view_index, 0, keepdims=False).reshape(
            slab_tiles, group_rows
        )
        projection, ray_sum = (
            lax.psum(projection.astype(jnp.bfloat16), "gx").astype(jnp.float32),
            lax.psum(ray_sum.astype(jnp.bfloat16), "gx").astype(jnp.float32),
        )
        residual = ((target - projection) / (ray_sum + 1.0)).astype(jnp.bfloat16)

        def backward(index, carry):
            change, voxel_sum = carry
            voxels, detector, chosen, weight = gather_group(index)
            product = jnp.einsum(
                "ejk,ej->ek",
                weight_blocks[chosen],
                residual[detector],
                preferred_element_type=jnp.float32,
            )
            return (
                change.at[voxels].add(product * weight),
                voxel_sum.at[voxels].add(col_weight[chosen] * weight),
            )

        blank = jnp.zeros((voxel_tiles.shape[0], group_rows), jnp.float32)
        change, voxel_sum = lax.fori_loop(0, rounds, backward, (blank, blank))
        current = current + (change / (voxel_sum + 1.0)).reshape(current.shape)
    art_volume = jnp.maximum(current, 0.0)
    difference = art_volume - volume
    change_part = jnp.sum(difference * difference)
    change_total = None
    change_total = lax.psum(change_part, ("gz", "gx"))
    smooth = art_volume
    for sweep_index in range(TV_STEPS):
        padded = padded_2(smooth, (("gz", 0), ("gx", 1)), 1)
        slope = tv_grad(pad_depth(padded))
        slope_part = jnp.sum(slope * slope)
        if sweep_index == 0:
            slope_total = lax.psum(slope_part, ("gz", "gx"))
        else:
            slope_total = lax.psum(slope_part, ("gz", "gx"))
        change_total, scale_now = (
            change_total,
            step_gain * jnp.sqrt(change_total) / jnp.sqrt(slope_total + norm_floor),
        )
        smooth = smooth - scale_now * slope
    return smooth


def solution(mesh):
    return jax.shard_map(
        body,
        mesh=mesh,
        in_specs=(
            P("gz", "gx", None),
            P(None, "gz", None),
            P(),
            P(),
            P(None, "gz", "gx"),
            P(None, "gz", "gx"),
            P(None, "gz", "gx"),
            P(None, "gz", "gx"),
        ),
        out_specs=P("gz", "gx", None),
        check_vma=False,
    )
```

profile of v0, /device:TPU:1, one launch (start us, length us, event | category | flops | bytes accessed | tf_op | source)
XLA Modules:
  0.0 943.3 jit_solution(2549535672975663778)
XLA Ops:
  17.6 13.5 %while.60 = (s32[]{:T(128)}, f32[512,128]{1,0:T(8,128)S(1)}, f32[512,128]{1,0:T(8,128)}, s32[]{:T(128)}, s32[512]{0:T(512)S(1)}, /*index=5*/s32[512]{0:T(512)S(1...) while((s32[]{:T(128)}, f32[512,128]{1,0:T(8,128)S(1)}, ...), condition=%wide.region_4.5_spmd.clone, body=%wide.region_1.4_spmd.clone.sunk | while | flops 4265478 | bytes 13388487 | solution.py:92
  17.7 3.0 gather_fusion
  21.5 4.4 fusion.99
  28.1 3.1 scatter_custom_fusion.43
  36.0 180.4 %all-reduce.12.cloned.1.call-done = (bf16[512,128]{1,0:T(8,128)(2,1)}, bf16[512,128]{1,0:T(8,128)(2,1)}) async-done(((bf16[512,128]{1,0:T(8,128)(2,1)}, bf16[512,128]{1,0:T(8,128)(2,1)}), (bf16[512,128]{1,0:T(8,128)(2,1)}, bf16[512,128]{1,0:T(8,128)(2,1)})) %all-reduce.12.cloned.1.call-update) | async-done | bytes 262160 | tf_op jit(solution)/shard_map/psum | solution.py:98
  219.1 14.2 %while.61 = (s32[]{:T(128)}, f32[1024,128]{1,0:T(8,128)}, f32[1024,128]{1,0:T(8,128)}, s32[]{:T(128)}, s32[512]{0:T(512)S(1)}, /*index=5*/s32[512]{0:T(512)S(1)}...) while((s32[]{:T(128)}, f32[1024,128]{1,0:T(8,128)}, ...), condition=%wide.region_11.12_spmd.clone, body=%wide.region_8.11_spmd.clone.sunk | while | flops 4265478 | bytes 13912775 | solution.py:117
  223.0 3.4 fusion.104
  227.0 3.1 scatter_custom_fusion.46
  230.1 3.3 scatter_custom_fusion.47
  241.9 14.9 %while.62 = (s32[]{:T(128)}, f32[512,128]{1,0:T(8,128)}, f32[512,128]{1,0:T(8,128)}, s32[]{:T(128)}, s32[512]{0:T(512)S(1)}, /*index=5*/s32[512]{0:T(512)S(1)}, ...) while((s32[]{:T(128)}, f32[512,128]{1,0:T(8,128)}, ...), condition=%wide.region_15.16_spmd.clone, body=%wide.region_12.15_spmd.clone.sunk | while | flops 4265478 | bytes 13388487 | solution.py:92
  245.7 4.4 fusion.109
  253.7 3.1 scatter_custom_fusion.51
  260.8 227.2 %all-reduce.10.cloned.1.call-done = (bf16[512,128]{1,0:T(8,128)(2,1)}, bf16[512,128]{1,0:T(8,128)(2,1)}) async-done(((bf16[512,128]{1,0:T(8,128)(2,1)}, bf16[512,128]{1,0:T(8,128)(2,1)}), (bf16[512,128]{1,0:T(8,128)(2,1)}, bf16[512,128]{1,0:T(8,128)(2,1)})) %all-reduce.10.cloned.1.call-update) | async-done | bytes 262160 | tf_op jit(solution)/shard_map/psum | solution.py:98
  490.0 12.7 %while.63 = (s32[]{:T(128)}, f32[1024,128]{1,0:T(8,128)S(1)}, f32[1024,128]{1,0:T(8,128)}, s32[]{:T(128)}, s32[512]{0:T(512)S(1)}, /*index=5*/s32[512]{0:T(512)S...) while((s32[]{:T(128)}, f32[1024,128]{1,0:T(8,128)S(1)}, ...), condition=%wide.region_21.22_spmd.clone, body=%wide.region_18.21_spmd.clone.sunk | while | flops 4265478 | bytes 13912775 | solution.py:117
  493.8 3.4 fusion.114
  499.4 3.3 scatter_custom_fusion.55
  504.9 8.1 collective-permute-start
  514.9 3.1 collective-permute-done.1
  521.3 3.4 collective-permute-done.3
  527.9 113.9 %all-reduce.4 = (f32[]{:T(128)}, f32[]{:T(128)}) all-reduce(f32[]{:T(128)} %get-tuple-element.839, f32[]{:T(128)} %get-tuple-element.837), channel_id=1, replica_groups=mesh['gz'=8,'gx'=32] {'gz','gx'}, use_global_device_ids=true, to_apply=%region_23.24 | all-reduce | flops 2 | bytes 16 | tf_op jit(solution)/shard_map/psum | solution.py:123
  643.4 3.5 collective-permute-start.4
  648.9 3.1 collective-permute-done.5
  654.8 3.6 collective-permute-done.7
  661.7 77.6 %psum.69 = f32[]{:T(128)} all-reduce(f32[]{:T(128)} %get-tuple-element.833), channel_id=1, replica_groups=mesh['gz'=8,'gx'=32] {'gz','gx'}, use_global_device_ids=true, to_apply=%region_27.28 | all-reduce | flops 1 | bytes 8 | tf_op jit(solution)/shard_map/psum | solution.py:132
  740.1 3.5 collective-permute-start.8
  745.5 3.1 collective-permute-done.9
  751.6 3.4 collective-permute-done.11
  758.3 78.8 %psum.70 = f32[]{:T(128)} all-reduce(f32[]{:T(128)} %get-tuple-element.829), channel_id=1, replica_groups=mesh['gz'=8,'gx'=32] {'gz','gx'}, use_global_device_ids=true, to_apply=%region_29.30 | all-reduce | flops 1 | bytes 8 | tf_op jit(solution)/shard_map/psum | solution.py:132
  837.8 3.5 collective-permute-start.12
  843.3 3.1 collective-permute-done.13
  849.2 3.6 collective-permute-done.15
  856.0 78.8 %psum.71 = f32[]{:T(128)} all-reduce(f32[]{:T(128)} %get-tuple-element.825), channel_id=1, replica_groups=mesh['gz'=8,'gx'=32] {'gz','gx'}, use_global_device_ids=true, to_apply=%region_31.32 | all-reduce | flops 1 | bytes 8 | tf_op jit(solution)/shard_map/psum | solution.py:132
  (119 shorter events, 84.7 us)
Async XLA Ops:
  6.5 10.1 %copy-start.1 = (f32[32,16,256]{2,1,0:T(8,128)S(1)}, f32[32,16,256]{2,1,0:T(8,128)}, u32[]{:S(2)}) copy-start(f32[32,16,256]{2,1,0:T(8,128)} %param.16) | copy-start | bytes 1572868
  6.5 209.8 %all-reduce.12.cloned.1.call-start = ((), (), s32[]{:S(2)}) async-start(), calls=%async_computation.1 | async-start | bytes 524288 | tf_op jit(solution)/shard_map/psum | solution.py:98
  14.3 2.6 copy-start.3
  14.3 2.6 copy-start.4
  14.3 3.4 copy-start
  33.4 454.6 %all-reduce.10.cloned.1.call-start = ((), (), s32[]{:S(2)}) async-start(), calls=%async_computation | async-start | bytes 524288 | tf_op jit(solution)/shard_map/psum | solution.py:98
  502.7 1.3 copy-start.2
  504.9 10.0 %collective-permute-start = (f32[1,16,256]{2,1,0:T(8,128)S(1)}, f32[1,16,256]{2,1,0:T(8,128)S(1)}, u32[]{:S(2)}, u32[]{:S(2)}) collective-permute-start(f32[1,16,256]{2,1,0:T(8,128)S(1)} %get-tuple-element.879), channel_id=1, source_target_pairs={{0,32},{32,64},{64,96},{96,128},{128,160},{160,192},{192,224},{1,3... | collective-permute-start | bytes 49160 | tf_op jit(solution)/shard_map/ppermute | solution.py:21
  513.0 5.1 collective-permute-start.1
  518.1 3.3 collective-permute-start.2
  520.0 4.7 collective-permute-start.3
  643.4 5.5 collective-permute-start.4
  647.0 5.1 collective-permute-start.5
  652.1 2.7 collective-permute-start.6
  653.5 4.9 collective-permute-start.7
  740.1 5.4 collective-permute-start.8
  743.6 5.1 collective-permute-start.9
  748.7 2.9 collective-permute-start.10
  750.1 4.9 collective-permute-start.11
  837.8 5.4 collective-permute-start.12
  841.3 5.1 collective-permute-start.13
  846.5 2.7 collective-permute-start.14
  847.9 4.9 collective-permute-start.15
Sparse Core Ops, SparseCore 0:
  33.6 182.7 all-reduce.11
  260.1 227.8 all-reduce.9
where the time goes:
time: 946 us; the launch traced here: 943 us
  waiting for transfers between devices  434 us (46%)
  blocking collectives  349 us (37%)
  other arithmetic  55.2 us (6%)
  starting transfers between devices  37.9 us (4%)
  local copies, waits for them, and re-layouts  28.9 us (3%)
  between operations  22.3 us (2%)
  matrix products  15.6 us (2%)
    psum x2, waiting for transfers between devices, body(): lax.psum(ray_sum.astype(jnp.bfloat16), 'gx').astype(jnp.float32)  408 us
    psum x3, blocking collectives, body(): slope_total = lax.psum(slope_part, ('gz', 'gx'))  235 us
    psum x1, blocking collectives, body(): change_total = lax.psum(change_part, ('gz', 'gx'))  114 us
    ppermute x8, waiting for transfers between devices, padded_2(): lax.ppermute(head, axis, [((i + 1) % count, i) for i in range(ends)])  26.5 us
    ppermute x8, starting transfers between devices, padded_2(): lax.ppermute(tail, axis, [(i, (i + 1) % count) for i in range(ends)])  24.8 us
  transfers between devices with their start and end apart: 18, of which 10 were waited for; matrix products, arithmetic and copies ran while one was open for 0% of the time, Pallas kernels for 0%

commit v1 on v0

--- a/solution.py
+++ b/solution.py
@@ -129,7 +129,9 @@
         if sweep_index == 0:
             slope_total = lax.psum(slope_part, ("gz", "gx"))
         else:
-            slope_total = lax.psum(slope_part, ("gz", "gx"))
+            slope_total = slope_part
+            for mesh_axis in ("gx", "gz"):
+                slope_total = lax.psum(slope_total, mesh_axis)
         change_total, scale_now = (
             change_total,
             step_gain * jnp.sqrt(change_total) / jnp.sqrt(slope_total + norm_floor),

time: 946 us -> 975 us (1.031); the launches traced: 943 us -> 956 us
  blocking collectives: 349 us -> 364 us
    psum x3 -> x6, blocking collectives: 235 us -> 251 us  [body(): slope_total = lax.psum(slope_total, mesh_axis)]
where the time goes in v1:
time: 975 us; the launch traced here: 956 us
  waiting for transfers between devices  432 us (44%)
  blocking collectives  364 us (37%)
  other arithmetic  55.1 us (6%)
  starting transfers between devices  37.7 us (4%)
  local copies, waits for them, and re-layouts  28.8 us (3%)
  between operations  22.5 us (2%)
  matrix products  15.6 us (2%)
    psum x2, waiting for transfers between devices, body(): lax.psum(ray_sum.astype(jnp.bfloat16), 'gx').astype(jnp.float32)  407 us
    psum x6, blocking collectives, body(): slope_total = lax.psum(slope_total, mesh_axis)  251 us
    psum x1, blocking collectives, body(): change_total = lax.psum(change_part, ('gz', 'gx'))  114 us
    ppermute x8, waiting for transfers between devices, padded_2(): lax.ppermute(head, axis, [((i + 1) % count, i) for i in range(ends)])  25 us
    ppermute x8, starting transfers between devices, padded_2(): lax.ppermute(tail, axis, [(i, (i + 1) % count) for i in range(ends)])  23.6 us
  transfers between devices with their start and end apart: 18, of which 10 were waited for; matrix products, arithmetic and copies ran while one was open for 0% of the time, Pallas kernels for 0%

profile of v1, /device:TPU:1, one launch (start us, length us, event | category | flops | bytes accessed | tf_op | source)
XLA Modules:
  0.0 956.3 jit_solution(11946203479004918018)
XLA Ops:
  18.0 13.5 %while.60 = (s32[]{:T(128)}, f32[512,128]{1,0:T(8,128)S(1)}, f32[512,128]{1,0:T(8,128)}, s32[]{:T(128)}, s32[512]{0:T(512)S(1)}, /*index=5*/s32[512]{0:T(512)S(1...) while((s32[]{:T(128)}, f32[512,128]{1,0:T(8,128)S(1)}, ...), condition=%wide.region_4.5_spmd.clone, body=%wide.region_1.4_spmd.clone.sunk | while | flops 4265478 | bytes 13388487 | solution.py:92
  18.1 3.0 gather_fusion
  21.8 4.4 fusion.99
  28.4 3.1 scatter_custom_fusion.43
  36.2 180.4 %all-reduce.12.cloned.1.call-done = (bf16[512,128]{1,0:T(8,128)(2,1)}, bf16[512,128]{1,0:T(8,128)(2,1)}) async-done(((bf16[512,128]{1,0:T(8,128)(2,1)}, bf16[512,128]{1,0:T(8,128)(2,1)}), (bf16[512,128]{1,0:T(8,128)(2,1)}, bf16[512,128]{1,0:T(8,128)(2,1)})) %all-reduce.12.cloned.1.call-update) | async-done | bytes 262160 | tf_op jit(solution)/shard_map/psum | solution.py:98
  219.4 14.2 %while.61 = (s32[]{:T(128)}, f32[1024,128]{1,0:T(8,128)}, f32[1024,128]{1,0:T(8,128)}, s32[]{:T(128)}, s32[512]{0:T(512)S(1)}, /*index=5*/s32[512]{0:T(512)S(1)}...) while((s32[]{:T(128)}, f32[1024,128]{1,0:T(8,128)}, ...), condition=%wide.region_11.12_spmd.clone, body=%wide.region_8.11_spmd.clone.sunk | while | flops 4265478 | bytes 13912775 | solution.py:117
  223.2 3.4 fusion.104
  227.3 3.1 scatter_custom_fusion.46
  230.3 3.3 scatter_custom_fusion.47
  242.1 14.8 %while.62 = (s32[]{:T(128)}, f32[512,128]{1,0:T(8,128)}, f32[512,128]{1,0:T(8,128)}, s32[]{:T(128)}, s32[512]{0:T(512)S(1)}, /*index=5*/s32[512]{0:T(512)S(1)}, ...) while((s32[]{:T(128)}, f32[512,128]{1,0:T(8,128)}, ...), condition=%wide.region_15.16_spmd.clone, body=%wide.region_12.15_spmd.clone.sunk | while | flops 4265478 | bytes 13388487 | solution.py:92
  245.9 4.4 fusion.109
  253.8 3.1 scatter_custom_fusion.51
  260.9 226.7 %all-reduce.10.cloned.1.call-done = (bf16[512,128]{1,0:T(8,128)(2,1)}, bf16[512,128]{1,0:T(8,128)(2,1)}) async-done(((bf16[512,128]{1,0:T(8,128)(2,1)}, bf16[512,128]{1,0:T(8,128)(2,1)}), (bf16[512,128]{1,0:T(8,128)(2,1)}, bf16[512,128]{1,0:T(8,128)(2,1)})) %all-reduce.10.cloned.1.call-update) | async-done | bytes 262160 | tf_op jit(solution)/shard_map/psum | solution.py:98
  489.6 12.6 %while.63 = (s32[]{:T(128)}, f32[1024,128]{1,0:T(8,128)S(1)}, f32[1024,128]{1,0:T(8,128)}, s32[]{:T(128)}, s32[512]{0:T(512)S(1)}, /*index=5*/s32[512]{0:T(512)S...) while((s32[]{:T(128)}, f32[1024,128]{1,0:T(8,128)S(1)}, ...), condition=%wide.region_21.22_spmd.clone, body=%wide.region_18.21_spmd.clone.sunk | while | flops 4265478 | bytes 13912775 | solution.py:117
  493.4 3.4 fusion.114
  498.9 3.3 scatter_custom_fusion.55
  504.3 8.1 collective-permute-start
  514.4 3.1 collective-permute-done.1
  520.8 3.4 collective-permute-done.3
  527.5 113.6 %all-reduce.4 = (f32[]{:T(128)}, f32[]{:T(128)}) all-reduce(f32[]{:T(128)} %get-tuple-element.839, f32[]{:T(128)} %get-tuple-element.837), channel_id=1, replica_groups=mesh['gz'=8,'gx'=32] {'gz','gx'}, use_global_device_ids=true, to_apply=%region_23.24 | all-reduce | flops 2 | bytes 16 | tf_op jit(solution)/shard_map/psum | solution.py:123
  642.5 3.5 collective-permute-start.4
  648.0 3.1 collective-permute-done.5
  653.9 3.6 collective-permute-done.7
  660.7 59.5 %psum.90 = f32[]{:T(128)} all-reduce(f32[]{:T(128)} %get-tuple-element.833), channel_id=1, replica_groups=mesh['gz'=8,'gx'=32] {'gx'}, use_global_device_ids=true, to_apply=%region_27.28 | all-reduce | flops 1 | bytes 8 | tf_op jit(solution)/shard_map/psum | solution.py:134
  720.2 26.3 %psum.91 = f32[]{:T(128)} all-reduce(f32[]{:T(128)} %psum.90), channel_id=1, replica_groups=mesh['gz'=8,'gx'=32] {'gz'}, use_global_device_ids=true, to_apply=%region_28.29 | all-reduce | flops 1 | bytes 8 | tf_op jit(solution)/shard_map/psum | solution.py:134
  757.2 3.1 collective-permute-done.11
  763.6 56.8 %psum.92 = f32[]{:T(128)} all-reduce(f32[]{:T(128)} %get-tuple-element.829), channel_id=1, replica_groups=mesh['gz'=8,'gx'=32] {'gx'}, use_global_device_ids=true, to_apply=%region_30.31 | all-reduce | flops 1 | bytes 8 | tf_op jit(solution)/shard_map/psum | solution.py:134
  820.4 25.6 %psum.93 = f32[]{:T(128)} all-reduce(f32[]{:T(128)} %psum.92), channel_id=1, replica_groups=mesh['gz'=8,'gx'=32] {'gz'}, use_global_device_ids=true, to_apply=%region_31.32 | all-reduce | flops 1 | bytes 8 | tf_op jit(solution)/shard_map/psum | solution.py:134
  853.8 3.6 collective-permute-start.14
  858.7 3.4 collective-permute-done.15
  865.3 56.3 %psum.94 = f32[]{:T(128)} all-reduce(f32[]{:T(128)} %get-tuple-element.825), channel_id=1, replica_groups=mesh['gz'=8,'gx'=32] {'gx'}, use_global_device_ids=true, to_apply=%region_33.34 | all-reduce | flops 1 | bytes 8 | tf_op jit(solution)/shard_map/psum | solution.py:134
  921.6 26.2 %psum.95 = f32[]{:T(128)} all-reduce(f32[]{:T(128)} %psum.94), channel_id=1, replica_groups=mesh['gz'=8,'gx'=32] {'gz'}, use_global_device_ids=true, to_apply=%region_34.35 | all-reduce | flops 1 | bytes 8 | tf_op jit(solution)/shard_map/psum | solution.py:134
  (122 shorter events, 93.0 us)
Async XLA Ops:
  6.5 10.5 %copy-start.1 = (f32[32,16,256]{2,1,0:T(8,128)S(1)}, f32[32,16,256]{2,1,0:T(8,128)}, u32[]{:S(2)}) copy-start(f32[32,16,256]{2,1,0:T(8,128)} %param.16) | copy-start | bytes 1572868
  6.5 210.1 %all-reduce.12.cloned.1.call-start = ((), (), s32[]{:S(2)}) async-start(), calls=%async_computation.1 | async-start | bytes 524288 | tf_op jit(solution)/shard_map/psum | solution.py:98
  14.7 2.6 copy-start.3
  14.7 2.6 copy-start.4
  14.7 3.4 copy-start
  33.8 453.8 %all-reduce.10.cloned.1.call-start = ((), (), s32[]{:S(2)}) async-start(), calls=%async_computation | async-start | bytes 524288 | tf_op jit(solution)/shard_map/psum | solution.py:98
  502.2 1.3 copy-start.2
  504.3 10.0 %collective-permute-start = (f32[1,16,256]{2,1,0:T(8,128)S(1)}, f32[1,16,256]{2,1,0:T(8,128)S(1)}, u32[]{:S(2)}, u32[]{:S(2)}) collective-permute-start(f32[1,16,256]{2,1,0:T(8,128)S(1)} %get-tuple-element.879), channel_id=1, source_target_pairs={{0,32},{32,64},{64,96},{96,128},{128,160},{160,192},{192,224},{1,3... | collective-permute-start | bytes 49160 | tf_op jit(solution)/shard_map/ppermute | solution.py:21
  512.4 5.1 collective-permute-start.1
  517.5 3.3 collective-permute-start.2
  519.5 4.7 collective-permute-start.3
  642.5 5.5 collective-permute-start.4
  646.1 5.1 collective-permute-start.5
  651.2 2.7 collective-permute-start.6
  652.5 4.9 collective-permute-start.7
  747.3 4.3 collective-permute-start.8
  749.2 5.1 collective-permute-start.9
  754.3 2.8 collective-permute-start.10
  755.6 4.7 collective-permute-start.11
  846.7 4.3 collective-permute-start.12
  848.6 5.1 collective-permute-start.13
  853.8 4.9 collective-permute-start.14
  857.3 4.7 collective-permute-start.15
Sparse Core Ops, SparseCore 0:
  33.9 182.6 all-reduce.11
  260.3 227.3 all-reduce.9
